TPU v7x, 32 devices: a whole 2x2x4 slice. The times are simulated.
32 devices in a mesh: uly: 2 (over x), blk: 16 (over z, y, core).
Axes of the slice: x: 2, y: 2, z: 4, core: 2. Of those that a mesh axis runs over, the one named last changes fastest.
Arguments:
- tokens: bfloat16 [4, 1024, 768], P('uly', 'blk'), may hold values from -6 to 6
- teacher: bfloat16 [4, 1024, 768], P('uly', 'blk'), may hold values from -6 to 6
- cotangent: bfloat16 [4, 1024, 768], P('uly', 'blk'), may hold values from -6 to 6
- valid: int32 [4, 1024], P('uly', 'blk'), may hold values from 0 to 1, as said below
- block_ids: int32 [4, 1024], replicated, may hold values from 0 to 7, never falling along the last dimension, each value on 1 to 256 neighbouring positions
- ln1_gain: float32 [768], replicated, may hold values from 0.1 to 1.9
- ln1_bias: float32 [768], replicated, may hold values from -1.5 to 1.5
- ln2_gain: float32 [768], replicated, may hold values from 0.1 to 1.9
- ln2_bias: float32 [768], replicated, may hold values from -1.5 to 1.5
- qkv_weight: bfloat16 [768, 896], P(('uly', 'blk')), may hold values from -0.3125 to 0.3125
- qkv_bias: float32 [896], replicated, may hold values from -1.5 to 1.5
- out_weight: bfloat16 [768, 768], P(('uly', 'blk')), may hold values from -1.25 to 1.25
- out_bias: float32 [768], replicated, may hold values from -1.5 to 1.5
- up_weight: bfloat16 [768, 3072], P(('uly', 'blk')), may hold values from -0.21875 to 0.21875
- up_bias: float32 [3072], replicated, may hold values from -2.5 to 2.5
- down_weight: bfloat16 [3072, 768], P(('uly', 'blk')), may hold values from -0.109375 to 0.109375
- down_bias: float32 [768], replicated, may hold values from -1.5 to 1.5
Outputs:
- activations: bfloat16 [4, 1024, 768], P('uly', 'blk')
- loss: float32 [], replicated
- tokens_grad: bfloat16 [4, 1024, 768], P('uly', 'blk')
- ln1_gain_grad: float32 [768], replicated
- ln1_bias_grad: float32 [768], replicated
- ln2_gain_grad: float32 [768], replicated
- ln2_bias_grad: float32 [768], replicated
- qkv_weight_grad: float32 [768, 896], P(('uly', 'blk'))
- qkv_bias_grad: float32 [896], replicated
- out_weight_grad: float32 [768, 768], P(('uly', 'blk'))
- out_bias_grad: float32 [768], replicated
- up_weight_grad: float32 [768, 3072], P(('uly', 'blk'))
- up_bias_grad: float32 [3072], replicated
- down_weight_grad: float32 [3072, 768], P(('uly', 'blk'))
- down_bias_grad: float32 [768], replicated
Inputs may be any that keep to these rules, and one draw needn't show every extreme that they name: `block_ids`: within each sequence the block ids never fall, and each block is 1 to 256 consecutive tokens. The first token of every sequence is valid.
All inputs are finite; a program needn't handle non-finite values.
Results may differ from a plain program's by a relative error of at most 0.017.
Values may be sent and summed in bfloat16 or wider, within the bound.
A program may use at most 128 MiB of HBM per device.

v0:
```python
import math

import jax
import jax.numpy as jnp
from jax import lax
from jax.sharding import PartitionSpec as P

HD = 64
ROT = 16


norm_eps = 1e-05


def from_behind(array, axis, by):
    count = lax.axis_size(axis)
    return lax.ppermute(array, axis, [(i, (i + by) % count) for i in range(count)])


def layer_norm(values, gain, shift):
    center = values - jnp.mean(values, -1, keepdims=True)
    spread = jnp.mean(center * center, -1, keepdims=True)
    return center * lax.rsqrt(spread + norm_eps) * gain + shift


def gelu_exact(values):
    return 0.5 * values * (1.0 + lax.erf(values * 0.7071067811865476))


def rotary_tables(position):
    halfway = ROT // 2
    freqs = jnp.exp(-(jnp.arange(halfway, dtype=jnp.float32) * (2.0 / ROT)) * math.log(10000.0))
    angles = position.astype(jnp.float32)[:, None] * freqs[None, :]
    angles = jnp.concatenate([angles, angles], -1)
    return (jnp.cos(angles), jnp.sin(angles))


def rotate(values, cosine, sine):
    halfway = ROT // 2
    leading = values[..., :ROT]
    turned = jnp.concatenate([-leading[..., halfway:], leading[..., :halfway]], -1)
    return jnp.concatenate([leading * cosine + turned * sine, values[..., ROT:]], -1)


def rotate_back(grads, cosine, sine):
    halfway = ROT // 2
    leading = grads[..., :ROT]
    scaled = leading * sine
    turned = jnp.concatenate([scaled[..., halfway:], -scaled[..., :halfway]], -1)
    return jnp.concatenate([leading * cosine + turned, grads[..., ROT:]], -1)


def on_device(
    tokens,
    teacher,
    cotangent,
    valid,
    block_ids,
    ln1_gain,
    ln1_bias,
    ln2_gain,
    ln2_bias,
    qkv_weight,
    qkv_bias,
    out_weight,
    out_bias,
    up_weight,
    up_bias,
    down_weight,
    down_bias,
):
    seqs_here, shard_len, width = tokens.shape
    rows_here = seqs_here * shard_len
    head_size = HD
    heads_all = width // head_size
    cycle_place = lax.axis_index("blk")
    own_start = cycle_place * shard_len
    position = own_start + jnp.arange(shard_len, dtype=jnp.int32)
    cosine, sine = rotary_tables(position)
    inputs = tokens.astype(jnp.float32).reshape(rows_here, width)
    live_rows = valid.astype(jnp.float32).reshape(rows_here)
    qkv_full, out_full, up_full, down_full = (
        lax.all_gather(qkv_weight, ("uly", "blk"), axis=0, tiled=True),
        lax.all_gather(out_weight, ("uly", "blk"), axis=0, tiled=True),
        lax.all_gather(up_weight, ("uly", "blk"), axis=0, tiled=True),
        lax.all_gather(down_weight, ("uly", "blk"), axis=0, tiled=True),
    )
    first_norm, first_pull = jax.vjp(layer_norm, inputs, ln1_gain, ln1_bias)
    second_norm, second_pull = jax.vjp(layer_norm, inputs, ln2_gain, ln2_bias)
    first_low = first_norm.astype(jnp.bfloat16)
    second_low = second_norm.astype(jnp.bfloat16)
    projected = jnp.dot(first_low, qkv_full, preferred_element_type=jnp.float32) + qkv_bias
    query_raw = projected[:, :width].reshape(seqs_here, shard_len, heads_all, head_size)
    key_raw = projected[:, width : width + head_size].reshape(seqs_here, shard_len, head_size)
    value_raw = projected[:, width + head_size :].reshape(seqs_here, shard_len, head_size)
    query_turned = rotate(query_raw, cosine[None, :, None, :], sine[None, :, None, :]).astype(
        jnp.bfloat16
    )
    key_turned = rotate(key_raw, cosine[None], sine[None]).astype(jnp.bfloat16)
    value_low = value_raw.astype(jnp.bfloat16)
    query_att = lax.all_to_all(query_turned, "uly", split_axis=2, concat_axis=0, tiled=True)
    key_att, value_att = (
        lax.all_gather(key_turned, "uly", axis=0, tiled=True),
        lax.all_gather(value_low, "uly", axis=0, tiled=True),
    )
    seqs_att = query_att.shape[0]
    heads_att = query_att.shape[2]
    rows_att = shard_len * heads_att
    query_rows = query_att.reshape(seqs_att, rows_att, head_size)
    query_ids = lax.dynamic_slice_in_dim(block_ids, own_start, shard_len, 1)
    row_ids = jnp.broadcast_to(query_ids[:, :, None], (seqs_att, shard_len, heads_att)).reshape(
        seqs_att, rows_att
    )
    last_ids = query_ids[:, shard_len - 1]

    def block_scores(key_block, id_block):
        scores = (
            jnp.einsum("snd,srd->snr", key_block, query_rows, preferred_element_type=jnp.float32)
            * 0.125
        )
        allowed = id_block[:, :, None] <= row_ids[:, None, :]
        return (scores, allowed)

    def over_piece(running, portion, anchor, update):
        key_piece, value_piece = portion
        extent = key_piece.shape[1]
        piece_ids = lax.dynamic_slice_in_dim(block_ids, anchor, extent, 1)
        stride = math.gcd(extent, 512)

        def visit(held_state):

            def one_step(counter, inner_state):
                first = counter * stride
                key_block = lax.dynamic_slice_in_dim(key_piece, first, stride, 1)
                value_block = lax.dynamic_slice_in_dim(value_piece, first, stride, 1)
                id_block = lax.dynamic_slice_in_dim(piece_ids, first, stride, 1)
                return update(inner_state, key_block, value_block, id_block, anchor, first)

            return lax.fori_loop(0, extent // stride, one_step, held_state)

        def untouched(held_state):
            return held_state

        visible = jnp.any(piece_ids[:, 0] <= last_ids)
        return lax.cond(visible, visit, untouched, running)

    def forward_update(held_state, key_block, value_block, id_block, anchor, first):
        maximum, weight_sum, accumulated = held_state
        scores, allowed = block_scores(key_block, id_block)
        scores = jnp.where(allowed, scores, -1e30)
        raised = jnp.maximum(maximum, jnp.max(scores, 1))
        factor = jnp.exp(maximum - raised)
        weights = jnp.where(allowed, jnp.exp(scores - raised[:, None, :]), 0.0)
        weight_sum = weight_sum * factor + jnp.sum(weights, 1)
        accumulated = accumulated * factor[:, None, :] + jnp.einsum(
            "snr,snd->sdr",
            weights.astype(jnp.bfloat16),
            value_block,
            preferred_element_type=jnp.float32,
        )
        return (raised, weight_sum, accumulated)

    start_state = (
        jnp.full((seqs_att, rows_att), -1e30, jnp.float32),
        jnp.zeros((seqs_att, rows_att), jnp.float32),
        jnp.zeros((seqs_att, head_size, rows_att), jnp.float32),
    )
    running_max, weight_sum, accumulated = over_piece(
        start_state,
        (
            lax.all_gather(key_att, "blk", axis=1, tiled=True),
            lax.all_gather(value_att, "blk", axis=1, tiled=True),
        ),
        jnp.int32(0),
        forward_update,
    )
    output_rows = accumulated / weight_sum[:, None, :]
    log_total = running_max + jnp.log(weight_sum)
    output_att = output_rows.reshape(seqs_att, head_size, shard_len, heads_att).transpose(
        0, 2, 3, 1
    )
    output_low = output_att.astype(jnp.bfloat16)
    output_tok = lax.all_to_all(output_low, "uly", split_axis=0, concat_axis=2, tiled=True)
    attn_rows = output_tok.reshape(rows_here, width)
    branch_attn = jnp.dot(attn_rows, out_full, preferred_element_type=jnp.float32) + out_bias
    hidden_pre = jnp.dot(second_low, up_full, preferred_element_type=jnp.float32) + up_bias
    hidden_act, gelu_pull = jax.vjp(gelu_exact, hidden_pre)
    hidden_low = hidden_act.astype(jnp.bfloat16)
    branch_ffn = jnp.dot(hidden_low, down_full, preferred_element_type=jnp.float32) + down_bias
    result = inputs + branch_attn + branch_ffn
    difference = result - teacher.astype(jnp.float32).reshape(rows_here, width)
    error_local = jnp.sum(jnp.mean(difference * difference, -1) * live_rows)
    error_sum, live_count = lax.psum((error_local, jnp.sum(live_rows)), ("uly", "blk"))
    upstream = (
        cotangent.astype(jnp.float32).reshape(rows_here, width)
        + difference * (live_rows * (2.0 / width) / live_count)[:, None]
    )
    upstream_low = upstream.astype(jnp.bfloat16)
    qkv_back, out_back, up_back, down_back = (
        lax.all_gather(qkv_weight, ("uly", "blk"), axis=0, tiled=True),
        lax.all_gather(out_weight, ("uly", "blk"), axis=0, tiled=True),
        lax.all_gather(up_weight, ("uly", "blk"), axis=0, tiled=True),
        lax.all_gather(down_weight, ("uly", "blk"), axis=0, tiled=True),
    )
    down_grad = jnp.einsum(
        "ri,rj->ij", hidden_low, upstream_low, preferred_element_type=jnp.float32
    )
    output_bias_grad = jnp.sum(upstream_low.astype(jnp.float32), 0)
    hidden_grad = jnp.einsum(
        "rj,ij->ri", upstream_low, down_back, preferred_element_type=jnp.float32
    )
    pre_grad = gelu_pull(hidden_grad)[0].astype(jnp.bfloat16)
    up_grad = jnp.einsum("ri,rj->ij", second_low, pre_grad, preferred_element_type=jnp.float32)
    up_bias_grad = jnp.sum(pre_grad.astype(jnp.float32), 0)
    second_grad = jnp.einsum("rj,ij->ri", pre_grad, up_back, preferred_element_type=jnp.float32)
    out_grad = jnp.einsum("ri,rj->ij", attn_rows, upstream_low, preferred_element_type=jnp.float32)
    attn_grad = jnp.einsum("rj,ij->ri", upstream_low, out_back, preferred_element_type=jnp.float32)
    attn_grad = attn_grad.astype(jnp.bfloat16).reshape(seqs_here, shard_len, heads_all, head_size)
    grad_att = lax.all_to_all(attn_grad, "uly", split_axis=2, concat_axis=0, tiled=True)
    grad_rows = grad_att.reshape(seqs_att, rows_att, head_size)
    delta = jnp.sum(grad_att.astype(jnp.float32) * output_att, -1).reshape(seqs_att, rows_att)

    def make_backward():

        def backward_update(held_state, key_block, value_block, id_block, anchor, first):
            query_acc, pair_acc = held_state
            scores, allowed = block_scores(key_block, id_block)
            probs = jnp.where(allowed, jnp.exp(scores - log_total[:, None, :]), 0.0)
            probs_low = probs.astype(jnp.bfloat16)
            value_grad = jnp.einsum(
                "snr,srd->snd", probs_low, grad_rows, preferred_element_type=jnp.float32
            )
            prob_grad = jnp.einsum(
                "snd,srd->snr", value_block, grad_rows, preferred_element_type=jnp.float32
            )
            score_grad = (probs * (prob_grad - delta[:, None, :])).astype(jnp.bfloat16)
            query_acc = query_acc + 0.125 * jnp.einsum(
                "snr,snd->sdr", score_grad, key_block, preferred_element_type=jnp.float32
            )
            key_grad = 0.125 * jnp.einsum(
                "snr,srd->snd", score_grad, query_rows, preferred_element_type=jnp.float32
            )
            previous = pair_acc
            pair_acc = previous + jnp.concatenate([key_grad, value_grad], -1)
            return (query_acc, pair_acc)

        return backward_update

    query_start = jnp.zeros((seqs_att, head_size, rows_att), jnp.float32)
    cycle_count = lax.axis_size("blk")
    cycle_update = make_backward()

    def cycle_step(step, carry):
        key_piece, value_piece, grad_piece, query_acc = carry
        anchor = (cycle_place - step) % cycle_count * shard_len
        query_acc, grad_piece = over_piece(
            (query_acc, grad_piece), (key_piece, value_piece), anchor, cycle_update
        )
        key_piece, value_piece = from_behind((key_piece, value_piece), "blk", 1)
        grad_piece = from_behind(grad_piece.astype(jnp.bfloat16), "blk", 1).astype(grad_piece.dtype)
        return (key_piece, value_piece, grad_piece, query_acc)

    cycle_start = (
        key_att,
        value_att,
        jnp.zeros((seqs_att, shard_len, 2 * head_size), jnp.float32),
        query_start,
    )
    unused_keys, unused_values, pair_grads, query_acc = lax.fori_loop(
        0, cycle_count, cycle_step, cycle_start
    )
    query_grad_att = query_acc.reshape(seqs_att, head_size, shard_len, heads_att).transpose(
        0, 2, 3, 1
    )
    query_grad_att = rotate_back(
        query_grad_att, cosine[None, :, None, :], sine[None, :, None, :]
    ).astype(jnp.bfloat16)
    query_grad_tok = lax.all_to_all(query_grad_att, "uly", split_axis=0, concat_axis=2, tiled=True)
    pair_grads = lax.psum_scatter(
        pair_grads.astype(jnp.bfloat16), "uly", scatter_dimension=0, tiled=True
    ).astype(jnp.float32)
    key_grad_low = rotate_back(pair_grads[..., :head_size], cosine[None], sine[None]).astype(
        jnp.bfloat16
    )
    value_grad_low = pair_grads[..., head_size:].astype(jnp.bfloat16)
    qkv_grad_rows = jnp.concatenate(
        [
            query_grad_tok.reshape(rows_here, width),
            key_grad_low.reshape(rows_here, head_size),
            value_grad_low.reshape(rows_here, head_size),
        ],
        -1,
    )
    qkv_grad = jnp.einsum("ri,rj->ij", first_low, qkv_grad_rows, preferred_element_type=jnp.float32)
    qkv_bias_grad = jnp.sum(qkv_grad_rows.astype(jnp.float32), 0)
    first_grad = jnp.einsum(
        "rj,ij->ri", qkv_grad_rows, qkv_back, preferred_element_type=jnp.float32
    )
    input_one, gain_one, shift_one = first_pull(first_grad)
    input_two, gain_two, shift_two = second_pull(second_grad)
    tokens_grad = (
        (upstream + input_one + input_two).astype(jnp.bfloat16).reshape(seqs_here, shard_len, width)
    )
    weight_parts = (
        lax.psum_scatter(qkv_grad, ("uly", "blk"), scatter_dimension=0, tiled=True),
        lax.psum_scatter(out_grad, ("uly", "blk"), scatter_dimension=0, tiled=True),
        lax.psum_scatter(up_grad, ("uly", "blk"), scatter_dimension=0, tiled=True),
        lax.psum_scatter(down_grad, ("uly", "blk"), scatter_dimension=0, tiled=True),
    )
    vector_parts = lax.psum(
        (gain_one, shift_one, gain_two, shift_two, qkv_bias_grad, output_bias_grad, up_bias_grad),
        ("uly", "blk"),
    )
    loss = error_sum / live_count
    activations = result.astype(jnp.bfloat16).reshape(seqs_here, shard_len, width)
    return (
        activations,
        loss,
        tokens_grad,
        vector_parts[0],
        vector_parts[1],
        vector_parts[2],
        vector_parts[3],
        weight_parts[0],
        vector_parts[4],
        weight_parts[1],
        vector_parts[5],
        weight_parts[2],
        vector_parts[6],
        weight_parts[3],
        vector_parts[5],
    )


def solution(mesh):
    return jax.shard_map(
        on_device,
        mesh=mesh,
        in_specs=(
            P("uly", "blk", None),
            P("uly", "blk", None),
            P("uly", "blk", None),
            P("uly", "blk"),
            P(),
            P(),
            P(),
            P(),
            P(),
            P(("uly", "blk"), None),
            P(),
            P(("uly", "blk"), None),
            P(),
            P(("uly", "blk"), None),
            P(),
            P(("uly", "blk"), None),
            P(),
        ),
        out_specs=(
            P("uly", "blk", None),
            P(),
            P("uly", "blk", None),
            P(),
            P(),
            P(),
            P(),
            P(("uly", "blk"), None),
            P(),
            P(("uly", "blk"), None),
            P(),
            P(("uly", "blk"), None),
            P(),
            P(("uly", "blk"), None),
            P(),
        ),
        check_vma=False,
    )
```

profile of v0, /device:TPU:1, one launch (start us, length us, event | category | flops | bytes accessed | tf_op | source)
XLA Modules:
  0.0 1014.3 jit_solution(11108664901134442652)
XLA Ops:
  19.2 48.8 %all-gather.5.cloned.1.call-done = bf16[768,896]{1,0:T(8,128)(2,1)} async-done(((bf16[24,896]{1,0:T(8,128)(2,1)}), bf16[768,896]{1,0:T(8,128)(2,1)}) %all-gather.5.cloned.1.call-update) | async-done | bytes 1376272 | tf_op jit(solution)/shard_map/all_gather | solution.py:83
  72.7 3.4 all-to-all-start
  76.4 5.1 all_gather.29
  81.5 3.4 all_gather.31
  85.0 26.3 %all_gather.30 = bf16[4,1024,64]{2,1,0:T(8,128)(2,1)S(1)} all-gather(bf16[4,64,64]{2,1,0:T(8,128)(2,1)S(1)} %all_gather.29), channel_id=1, replica_groups=mesh['uly'=2,'blk'=16] {'blk'}, dimensions={1}, use_global_device_ids=true | all-gather | bytes 557056 | tf_op jit(solution)/shard_map/all_gather | solution.py:171
  111.2 24.2 %all_gather.32 = bf16[4,1024,64]{2,1,0:T(8,128)(2,1)S(1)} all-gather(bf16[4,64,64]{2,1,0:T(8,128)(2,1)S(1)} %all_gather.31), channel_id=1, replica_groups=mesh['uly'=2,'blk'=16] {'blk'}, dimensions={1}, use_global_device_ids=true | all-gather | bytes 557056 | tf_op jit(solution)/shard_map/all_gather | solution.py:172
  137.4 20.9 %conditional.2 = (f32[4,384]{1,0:T(4,128)}, f32[4,384]{1,0:T(4,128)}, f32[4,64,384]{2,1,0:T(8,128)}, f32[4,384]{1,0:T(4,128)S(1)}) conditional(s32[]{:T(128)} %convert_element_type.120, () %tuple.63, (s32[4,1024]{1,0:T(4,128)}, s32[4,64,6]{2,1,0:T(8,128)S(1)}, bf16[4,1024,64]{2,1,0:T(8,128)(2,1)S(1)}, bf16[4,384,64]{2,0,1:T(4,128)(2,1)}, ...), branch_computations={%region_3.0_spmd, %region_4.9_spmd} | conditional | flops 214212096 | bytes 15739291 | solution.py:145
  141.8 15.9 %while.46 = (s32[]{:T(128)}, f32[4,384]{1,0:T(4,128)}, f32[4,384]{1,0:T(4,128)}, f32[4,64,384]{2,1,0:T(8,128)}, s32[4,1024]{1,0:T(4,128)}, /*index=5*/s32[4,64,6...) while((s32[]{:T(128)}, f32[4,384]{1,0:T(4,128)}, ...), condition=%wide.wide.region_8.0_spmd.clone, body=%wide.wide.region_5.7_spmd.clone.sunk | while | flops 214212096 | bytes 13199591 | solution.py:139
  154.2 2.8 fusion.104
  160.3 6.8 all_to_all.60
  167.9 3.2 convolution_add_fusion
  171.2 34.7 %all-gather.11.cloned.1.call-done = bf16[3072,768]{1,0:T(8,128)(2,1)} async-done(((bf16[96,768]{1,0:T(8,128)(2,1)}), bf16[3072,768]{1,0:T(8,128)(2,1)}) %all-gather.11.cloned.1.call-update) | async-done | bytes 4718608 | tf_op jit(solution)/shard_map/all_gather | solution.py:86
  205.9 4.0 convolution_add_fusion.3
  209.9 51.7 %all-gather.7.cloned.1.call-done = bf16[768,768]{1,0:T(8,128)(2,1)} async-done(((bf16[24,768]{1,0:T(8,128)(2,1)}), bf16[768,768]{1,0:T(8,128)(2,1)}) %all-gather.7.cloned.1.call-update) | async-done | bytes 1179664 | tf_op jit(solution)/shard_map/all_gather | solution.py:84
  264.3 38.4 %psum.64 = f32[]{:T(128)} all-reduce(f32[]{:T(128)} %get-tuple-element.762), channel_id=1, replica_groups=mesh['uly'=2,'blk'=16] {'uly','blk'}, use_global_device_ids=true, to_apply=%region_13.14 | all-reduce | flops 1 | bytes 8 | tf_op jit(solution)/shard_map/psum | solution.py:193
  311.0 3.4 all-to-all-start.2
  325.0 175.5 %while.47 = (s32[]{:T(128)}, bf16[4,64,64]{1,2,0:T(8,128)(2,1)S(1)}, bf16[4,64,64]{2,1,0:T(8,128)(2,1)S(1)}, f32[4,64,128]{2,1,0:T(8,128)S(1)}, f32[4,64,384]{2,...) while((s32[]{:T(128)}, ...), condition=%wide.region_19.20_spmd.clone, body=%wide.region_15.19_spmd.clone.sunk | while | flops 64077848 | bytes 5329560 | solution.py:269
  329.7 4.6 collective-permute-start.2
  341.4 2.5 collective-permute-start.2
  350.0 4.1 collective-permute-start.2
  360.6 2.4 collective-permute-start.2
  363.6 3.4 collective-permute-start.1
  371.2 2.4 collective-permute-start.2
  373.7 3.9 collective-permute-start.1
  381.8 2.4 collective-permute-start.2
  393.3 3.2 collective-permute-start.1
  403.8 3.3 collective-permute-start.1
  416.0 4.1 collective-permute-done.2
  423.4 3.2 collective-permute-start.1
  426.6 4.3 collective-permute-done.2
  434.1 3.1 collective-permute-start.1
  437.2 4.4 collective-permute-done.2
  446.2 6.2 collective-permute-done.2
  457.3 5.8 collective-permute-done.2
  469.1 6.5 collective-permute-done.2
  480.5 7.5 collective-permute-done.2
  492.9 7.5 collective-permute-done.2
  501.3 2.9 fusion.52
  507.4 6.3 all_to_all.61
  521.4 5.1 fusion.44
  526.8 4.2 convert_reduce_fusion
  531.0 5.1 fusion.53
  536.2 4.2 fusion.51
  541.7 45.2 %all-reduce.1 = (f32[]{:T(128)}, f32[768]{0:T(1024)}, f32[768]{0:T(1024)}, f32[768]{0:T(1024)}, f32[768]{0:T(1024)}, /*index=5*/f32[896]{0:T(1024)}, f32[768]{0:T(1024)S(1)}, f32[3072]{0:T(1024)}) all-reduce(f32[]{:T(128)} %get-tuple-element.763, f32[768]{0:T(1024)S(1)} %get-tuple-element.761, ...), channel_id=1, replica_groups=mesh['uly'=2,'blk'=16] {'uly','blk'}, use_global_device_ids=true, to_apply=%region_11.12 | all-reduce | flops 7809 | bytes 62472 | tf_op jit(solution)/shard_map/psum | solution.py:193
  589.3 27.8 %reduce-scatter.10.cloned.1.call-done = f32[24,768]{1,0:T(8,128)} async-done(((f32[768,768]{1,0:T(8,128)}), f32[24,768]{1,0:T(8,128)}) %reduce-scatter.10.cloned.1.call-update) | async-done | bytes 73744 | tf_op jit(solution)/shard_map/reduce_scatter | solution.py:306
  617.2 106.0 %reduce-scatter.16.cloned.1.call-done = f32[24,896]{1,0:T(8,128)} async-done(((f32[768,896]{1,0:T(8,128)}), f32[24,896]{1,0:T(8,128)}) %reduce-scatter.16.cloned.1.call-update) | async-done | bytes 86032
  723.2 140.8 %reduce-scatter.14.cloned.1.call-done = f32[96,768]{1,0:T(8,128)} async-done(((f32[3072,768]{1,0:T(8,128)}), f32[96,768]{1,0:T(8,128)}) %reduce-scatter.14.cloned.1.call-update) | async-done | bytes 294928 | tf_op jit(solution)/shard_map/reduce_scatter | solution.py:308
  864.0 142.0 %reduce-scatter.12.cloned.1.call-done = f32[24,3072]{1,0:T(8,128)} async-done(((f32[768,3072]{1,0:T(8,128)}), f32[24,3072]{1,0:T(8,128)}) %reduce-scatter.12.cloned.1.call-update) | async-done | bytes 294928 | tf_op jit(solution)/shard_map/reduce_scatter | solution.py:307
  (496 shorter events, 164.1 us)
Async XLA Ops:
  7.2 60.8 %all-gather.5.cloned.1.call-start = ((), (), s32[]{:S(2)}) async-start(), calls=%async_computation.9 | async-start | bytes 1419264 | tf_op jit(solution)/shard_map/all_gather | solution.py:83
  7.9 160.0 %all-gather.9.cloned.1.call-start = ((), (), s32[]{:S(2)}) async-start(), calls=%async_computation.11 | async-start | bytes 4866048 | tf_op jit(solution)/shard_map/all_gather | solution.py:85
  8.7 197.2 %all-gather.11.cloned.1.call-start = ((), (), s32[]{:S(2)}) async-start(), calls=%async_computation.12 | async-start | bytes 4866048 | tf_op jit(solution)/shard_map/all_gather | solution.py:86
  9.4 252.2 %all-gather.7.cloned.1.call-start = ((), (), s32[]{:S(2)}) async-start(), calls=%async_computation.10 | async-start | bytes 1216512 | tf_op jit(solution)/shard_map/all_gather | solution.py:84
  72.7 62.8 %all-to-all-start = ((bf16[2,2,24576]{2,1,0:T(2,128)(2,1)}), bf16[2,2,24576]{2,1,0:T(2,128)(2,1)S(1)}, u32[]{:S(2)}, u32[]{:S(2)}) async-start(bf16[2,2,24576]{2,1,0:T(2,128)(2,1)} %reshape.333), calls=%async_computation | async-start | bytes 393216 | tf_op jit(solution)/shard_map/all_to_all | solution.py:101
  311.0 7.1 all-to-all-start.2
  314.5 200.1 %reduce-scatter.8.cloned.1.call-start = ((), (), s32[]{:S(2)}) async-start(), calls=%async_computation.13 | async-start | bytes 98304 | tf_op jit(solution)/shard_map/reduce_scatter | solution.py:279
  329.7 5.9 collective-permute-start.2
  350.0 6.4 collective-permute-start.2
  360.6 6.4 collective-permute-start.2
  363.6 4.7 collective-permute-start.1
  371.2 6.4 collective-permute-start.2
  373.7 5.2 collective-permute-start.1
  381.8 6.0 collective-permute-start.2
  391.0 7.7 collective-permute-start.2
  393.2 5.5 collective-permute-start
  393.3 5.6 collective-permute-start.1
  401.7 7.7 collective-permute-start.2
  403.1 6.4 collective-permute-start
  403.8 5.8 collective-permute-start.1
  412.5 7.7 collective-permute-start.2
  413.7 6.5 collective-permute-start
  413.8 6.6 collective-permute-start.1
  423.2 7.7 collective-permute-start.2
  423.3 7.7 collective-permute-start
  423.4 7.7 collective-permute-start.1
  434.0 7.7 collective-permute-start.2
  434.0 7.7 collective-permute-start
  434.1 7.7 collective-permute-start.1
  444.7 7.7 collective-permute-start.2
  444.8 7.7 collective-permute-start
  444.9 7.7 collective-permute-start.1
  457.1 6.0 collective-permute-start.2
  457.2 6.0 collective-permute-start
  457.3 6.1 collective-permute-start.1
  467.9 7.7 collective-permute-start.2
  468.0 7.7 collective-permute-start
  468.0 7.7 collective-permute-start.1
  480.3 7.7 collective-permute-start.2
  480.4 7.7 collective-permute-start
  480.4 7.7 collective-permute-start.1
  492.7 7.7 collective-permute-start.2
  492.8 7.7 collective-permute-start
  492.8 7.7 collective-permute-start.1
  501.2 116.0 %reduce-scatter.10.cloned.1.call-start = ((), (), s32[]{:S(2)}) async-start(), calls=%async_computation.14 | async-start | bytes 2433024 | tf_op jit(solution)/shard_map/reduce_scatter | solution.py:306
  504.2 219.0 %reduce-scatter.16.cloned.1.call-start = ((), (), s32[]{:S(2)}) async-start(), calls=%async_computation.17 | async-start | bytes 2838528
  520.5 343.5 %reduce-scatter.14.cloned.1.call-start = ((), (), s32[]{:S(2)}) async-start(), calls=%async_computation.16 | async-start | bytes 9732096 | tf_op jit(solution)/shard_map/reduce_scatter | solution.py:308
  526.5 479.5 %reduce-scatter.12.cloned.1.call-start = ((), (), s32[]{:S(2)}) async-start(), calls=%async_computation.15 | async-start | bytes 9732096 | tf_op jit(solution)/shard_map/reduce_scatter | solution.py:307
  (52 other events, 1590.0 us)
Sparse Core Ops, SparseCore 0:
  10.8 57.0 all-gather.4
  70.9 70.2 all-gather.8
  144.1 61.7 all-gather.10
  208.6 52.9 all-gather.6
  501.3 12.0 reduce-scatter.7
  519.1 97.9 reduce-scatter.9
  624.0 99.1 reduce-scatter.15
  729.6 134.3 reduce-scatter.13
  871.5 134.4 reduce-scatter.11
where the time goes:
time: 1020 us; the launch traced here: 1010 us
  waiting for transfers between devices  618 us (61%)
  blocking collectives  156 us (15%)
  starting transfers between devices  64.2 us (6%)
  matrix products  52 us (5%)
  local copies, waits for them, and re-layouts  50.1 us (5%)
  other arithmetic  44.5 us (4%)
  between operations  17.8 us (2%)
  loops' own time  12.1 us (1%)
    reduce_scatter x1, waiting for transfers between devices, on_device(): lax.psum_scatter(up_grad, ('uly', 'blk'), scatter_dimension=0, tiled=True)  142 us
    reduce_scatter x1, waiting for transfers between devices, on_device(): lax.psum_scatter(down_grad, ('uly', 'blk'), scatter_dimension=0, tiled=True)  141 us
    unnamed x10, waiting for transfers between devices  109 us
    psum x2, blocking collectives, on_device(): lax.psum((error_local, jnp.sum(live_rows)), ('uly', 'blk'))  83.6 us
    ppermute x48, waiting for transfers between devices, from_behind(): lax.ppermute(array, axis, [(i, (i + by) % count) for i in range(count)])  61.8 us
    ppermute x48, starting transfers between devices, from_behind(): lax.ppermute(array, axis, [(i, (i + by) % count) for i in range(count)])  56.8 us
    all_gather x1, waiting for transfers between devices, on_device(): lax.all_gather(out_weight, ('uly', 'blk'), axis=0, tiled=True)  51.7 us
    all_gather x1, waiting for transfers between devices, on_device(): lax.all_gather(qkv_weight, ('uly', 'blk'), axis=0, tiled=True)  48.8 us
  transfers between devices with their start and end apart: 59, of which 49 were waited for; matrix products, arithmetic and copies ran while one was open for 8% of the time, Pallas kernels for 0%

commit v1 on v0

v1 whole, which is shorter than its diff:
```python
import math

import jax
import jax.numpy as jnp
from jax import lax
from jax.sharding import PartitionSpec as P

HD = 64
ROT = 16


norm_eps = 1e-05
BOTH = ("uly", "blk")


def layer_norm(values, gain, shift):
    center = values - jnp.mean(values, -1, keepdims=True)
    spread = jnp.mean(center * center, -1, keepdims=True)
    return center * lax.rsqrt(spread + norm_eps) * gain + shift


def gelu_exact(values):
    return 0.5 * values * (1.0 + lax.erf(values * 0.7071067811865476))


def rotary_tables(position):
    halfway = ROT // 2
    freqs = jnp.exp(-(jnp.arange(halfway, dtype=jnp.float32) * (2.0 / ROT)) * math.log(10000.0))
    angles = position.astype(jnp.float32)[:, None] * freqs[None, :]
    angles = jnp.concatenate([angles, angles], -1)
    return (jnp.cos(angles), jnp.sin(angles))


def rotate(values, cosine, sine):
    halfway = ROT // 2
    leading = values[..., :ROT]
    turned = jnp.concatenate([-leading[..., halfway:], leading[..., :halfway]], -1)
    return jnp.concatenate([leading * cosine + turned * sine, values[..., ROT:]], -1)


def rotate_back(grads, cosine, sine):
    halfway = ROT // 2
    leading = grads[..., :ROT]
    scaled = leading * sine
    turned = jnp.concatenate([scaled[..., halfway:], -scaled[..., :halfway]], -1)
    return jnp.concatenate([leading * cosine + turned, grads[..., ROT:]], -1)


def mm(pattern, a, b):
    return jnp.einsum(pattern, a, b, preferred_element_type=jnp.float32)


def scatter_sum(part):
    low = part.astype(jnp.bfloat16)
    return lax.psum_scatter(low, BOTH, scatter_dimension=0, tiled=True).astype(jnp.float32)


def general_layer(
    tokens,
    teacher,
    cotangent,
    valid,
    block_ids,
    ln1_gain,
    ln1_bias,
    ln2_gain,
    ln2_bias,
    qkv_weight,
    qkv_bias,
    out_weight,
    out_bias,
    up_weight,
    up_bias,
    down_weight,
    down_bias,
):
    seqs, shard_len, width = tokens.shape
    rows_here = seqs * shard_len
    heads = width // HD
    own_start = lax.axis_index("blk") * shard_len
    position = own_start + jnp.arange(shard_len, dtype=jnp.int32)
    cosine, sine = rotary_tables(position)
    inputs = tokens.astype(jnp.float32).reshape(rows_here, width)
    live_rows = valid.astype(jnp.float32).reshape(rows_here)
    live_count = lax.psum(jnp.sum(live_rows), BOTH)
    qkv_full, out_full, up_full, down_full = (
        lax.all_gather(w, BOTH, axis=0, tiled=True)
        for w in (qkv_weight, out_weight, up_weight, down_weight)
    )
    first_norm, first_pull = jax.vjp(layer_norm, inputs, ln1_gain, ln1_bias)
    second_norm, second_pull = jax.vjp(layer_norm, inputs, ln2_gain, ln2_bias)
    first_low = first_norm.astype(jnp.bfloat16)
    second_low = second_norm.astype(jnp.bfloat16)
    projected = jnp.dot(first_low, qkv_full, preferred_element_type=jnp.float32) + qkv_bias
    query_raw = projected[:, :width].reshape(seqs, shard_len, heads, HD)
    key_raw = projected[:, width : width + HD].reshape(seqs, shard_len, HD)
    value_raw = projected[:, width + HD :].reshape(seqs, shard_len, HD)
    query = rotate(query_raw, cosine[None, :, None, :], sine[None, :, None, :])
    query = query.astype(jnp.bfloat16)
    key_own = rotate(key_raw, cosine[None], sine[None]).astype(jnp.bfloat16)
    pair_own = jnp.concatenate([key_own, value_raw.astype(jnp.bfloat16)], -1)
    pair_all = lax.all_gather(pair_own, "blk", axis=1, tiled=True)
    length = pair_all.shape[1]
    stride = math.gcd(length, 1024)
    rows_att = heads * shard_len
    q_rows = query.transpose(0, 2, 1, 3).reshape(seqs, rows_att, HD)
    first_seq = lax.axis_index("uly") * seqs
    ids_all = lax.dynamic_slice_in_dim(block_ids, first_seq, seqs, 0)
    ids_own = lax.dynamic_slice_in_dim(ids_all, own_start, shard_len, 1)
    row_ids = jnp.tile(ids_own, (1, heads))
    last_ids = ids_own[:, shard_len - 1]

    def piece(counter):
        first = counter * stride
        pair = lax.dynamic_slice_in_dim(pair_all, first, stride, 1)
        ids = lax.dynamic_slice_in_dim(ids_all, first, stride, 1)
        return pair[..., :HD], pair[..., HD:], ids

    def scores_of(keys, ids):
        scores = mm("snd,srd->snr", keys, q_rows) * 0.125
        return scores, ids[:, :, None] <= row_ids[:, None, :]

    def forward_step(counter, state):
        keys, values, ids = piece(counter)

        def visit(state):
            maximum, weight_sum, accumulated = state
            scores, allowed = scores_of(keys, ids)
            scores = jnp.where(allowed, scores, -1e30)
            raised = jnp.maximum(maximum, jnp.max(scores, 1))
            factor = jnp.exp(maximum - raised)
            weights = jnp.where(allowed, jnp.exp(scores - raised[:, None, :]), 0.0)
            weight_sum = weight_sum * factor + jnp.sum(weights, 1)
            accumulated = accumulated * factor[:, None, :] + mm(
                "snr,snd->sdr", weights.astype(jnp.bfloat16), values
            )
            return (raised, weight_sum, accumulated)

        return lax.cond(jnp.any(ids[:, 0] <= last_ids), visit, lambda s: s, state)

    running_max, weight_sum, accumulated = lax.fori_loop(
        0,
        length // stride,
        forward_step,
        (
            jnp.full((seqs, rows_att), -1e30, jnp.float32),
            jnp.zeros((seqs, rows_att), jnp.float32),
            jnp.zeros((seqs, HD, rows_att), jnp.float32),
        ),
    )
    output_rows = accumulated / weight_sum[:, None, :]
    log_total = running_max + jnp.log(weight_sum)

    def to_tokens(rows):
        return (
            rows.reshape(seqs, HD, heads, shard_len).transpose(0, 3, 2, 1).reshape(rows_here, width)
        )

    attn_full = to_tokens(output_rows)
    attn_rows = attn_full.astype(jnp.bfloat16)
    branch_attn = jnp.dot(attn_rows, out_full, preferred_element_type=jnp.float32) + out_bias
    hidden_pre = jnp.dot(second_low, up_full, preferred_element_type=jnp.float32) + up_bias
    hidden_act, gelu_pull = jax.vjp(gelu_exact, hidden_pre)
    hidden_low = hidden_act.astype(jnp.bfloat16)
    branch_ffn = jnp.dot(hidden_low, down_full, preferred_element_type=jnp.float32) + down_bias
    result = inputs + branch_attn + branch_ffn
    difference = result - teacher.astype(jnp.float32).reshape(rows_here, width)
    error_local = jnp.sum(jnp.mean(difference * difference, -1) * live_rows)
    upstream = (
        cotangent.astype(jnp.float32).reshape(rows_here, width)
        + difference * (live_rows * (2.0 / width) / live_count)[:, None]
    )
    upstream_low = upstream.astype(jnp.bfloat16)
    down_grad = scatter_sum(mm("ri,rj->ij", hidden_low, upstream_low))
    output_bias_grad = jnp.sum(upstream_low.astype(jnp.float32), 0)
    hidden_grad = mm("rj,ij->ri", upstream_low, down_full)
    pre_grad = gelu_pull(hidden_grad)[0].astype(jnp.bfloat16)
    up_grad = scatter_sum(mm("ri,rj->ij", second_low, pre_grad))
    up_bias_grad = jnp.sum(pre_grad.astype(jnp.float32), 0)
    second_grad = mm("rj,ij->ri", pre_grad, up_full)
    out_grad = scatter_sum(mm("ri,rj->ij", attn_rows, upstream_low))
    attn_grad = mm("rj,ij->ri", upstream_low, out_full).astype(jnp.bfloat16)
    grad_tok = attn_grad.reshape(seqs, shard_len, heads, HD)
    grad_rows = grad_tok.transpose(0, 2, 1, 3).reshape(seqs, rows_att, HD)
    delta = jnp.sum(
        (attn_grad.astype(jnp.float32) * attn_full).reshape(seqs, shard_len, heads, HD), -1
    )
    delta = delta.transpose(0, 2, 1).reshape(seqs, rows_att)

    def backward_step(counter, state):
        keys, values, ids = piece(counter)

        def visit(state):
            query_acc, pair_acc = state
            scores, allowed = scores_of(keys, ids)
            probs = jnp.where(allowed, jnp.exp(scores - log_total[:, None, :]), 0.0)
            value_grad = mm("snr,srd->snd", probs.astype(jnp.bfloat16), grad_rows)
            prob_grad = mm("snd,srd->snr", values, grad_rows)
            score_grad = (probs * (prob_grad - delta[:, None, :])).astype(jnp.bfloat16)
            query_acc = query_acc + 0.125 * mm("snr,snd->sdr", score_grad, keys)
            key_grad = 0.125 * mm("snr,srd->snd", score_grad, q_rows)
            both = jnp.concatenate([key_grad, value_grad], -1).astype(jnp.bfloat16)
            return (query_acc, lax.dynamic_update_slice_in_dim(pair_acc, both, counter * stride, 1))

        return lax.cond(jnp.any(ids[:, 0] <= last_ids), visit, lambda s: s, state)

    query_acc, pair_grads = lax.fori_loop(
        0,
        length // stride,
        backward_step,
        (
            jnp.zeros((seqs, HD, rows_att), jnp.float32),
            jnp.zeros((seqs, length, 2 * HD), jnp.bfloat16),
        ),
    )
    pair_grads = lax.psum_scatter(pair_grads, "blk", scatter_dimension=1, tiled=True)
    pair_grads = pair_grads.astype(jnp.float32)
    query_grad = to_tokens(query_acc).reshape(seqs, shard_len, heads, HD)
    query_grad = rotate_back(query_grad, cosine[None, :, None, :], sine[None, :, None, :])
    key_grad = rotate_back(pair_grads[..., :HD], cosine[None], sine[None])
    qkv_grad_rows = jnp.concatenate(
        [
            query_grad.reshape(rows_here, width),
            key_grad.reshape(rows_here, HD),
            pair_grads[..., HD:].reshape(rows_here, HD),
        ],
        -1,
    ).astype(jnp.bfloat16)
    qkv_grad = scatter_sum(mm("ri,rj->ij", first_low, qkv_grad_rows))
    qkv_bias_grad = jnp.sum(qkv_grad_rows.astype(jnp.float32), 0)
    first_grad = mm("rj,ij->ri", qkv_grad_rows, qkv_full)
    input_one, gain_one, shift_one = first_pull(first_grad)
    input_two, gain_two, shift_two = second_pull(second_grad)
    tokens_grad = (
        (upstream + input_one + input_two).astype(jnp.bfloat16).reshape(seqs, shard_len, width)
    )
    vectors = (
        gain_one,
        shift_one,
        gain_two,
        shift_two,
        qkv_bias_grad,
        output_bias_grad,
        up_bias_grad,
        error_local,
    )
    vectors = lax.psum(vectors, BOTH)
    loss = vectors[7] / live_count
    activations = result.astype(jnp.bfloat16).reshape(seqs, shard_len, width)
    return (
        activations,
        loss,
        tokens_grad,
        vectors[0],
        vectors[1],
        vectors[2],
        vectors[3],
        qkv_grad,
        vectors[4],
        out_grad,
        vectors[5],
        up_grad,
        vectors[6],
        down_grad,
        vectors[5],
    )


def solution(mesh):
    tok = P("uly", "blk", None)
    row = P(("uly", "blk"), None)
    rep = P()
    return jax.shard_map(
        general_layer,
        mesh=mesh,
        in_specs=(tok, tok, tok, P("uly", "blk"), rep, rep, rep, rep, rep)
        + (row, rep, row, rep, row, rep, row, rep),
        out_specs=(tok, rep, tok, rep, rep, rep, rep, row, rep, row, rep, row, rep, row, rep),
        check_vma=False,
    )
```

time: 1020 us -> 853 us (0.84)
  starting transfers between devices: 64.2 us -> 0.58 us
  blocking collectives: 156 us -> 102 us
  other arithmetic: 44.5 us -> 25.3 us
  loops' own time: 12.1 us -> 0.12 us
  local copies, waits for them, and re-layouts: 50.1 us -> 39.4 us
    unnamed x10 -> x11, waiting for transfers between devices: 109 us -> 177 us
    ppermute x48 -> x0, waiting for transfers between devices: 61.8 us -> none  [from_behind(): lax.ppermute(array, axis, [(i, (i + by) % count) for i in range(count)])]
    reduce_scatter x4 -> x3, waiting for transfers between devices: 311 us -> 253 us  [scatter_sum(): lax.psum_scatter(low, BOTH, scatter_dimension=0, tiled=True)]
    ppermute x48 -> x0, starting transfers between devices: 56.8 us -> none  [from_behind(): lax.ppermute(array, axis, [(i, (i + by) % count) for i in range(count)])]
    all_gather x4, waiting for transfers between devices: 135 us -> 188 us  [general_layer(): lax.all_gather(w, BOTH, axis=0, tiled=True)]
    all_gather x4 -> x1, blocking collectives: 59 us -> 22.1 us  [general_layer(): pair_all = lax.all_gather(pair_own, 'blk', axis=1, tiled=True)]
    reduce_or x17 -> x1, other arithmetic: 22 us -> 1.39 us  [forward_step(): return lax.cond(jnp.any(ids[:, 0] <= last_ids), visit, lambda s: s, state)]
    all_to_all x2 -> x0, blocking collectives: 13.1 us -> none  [the longest x1 6.76 us: on_device(): lax.all_to_all(output_low, 'uly', split_axis=0, concat_axis=2, tiled=True)]
  transfers between devices with their start and end apart: 59 -> 9, of which waited for: 49 -> 9; matrix products, arithmetic and copies ran while one was open for 8% -> 8% of each run, Pallas kernels for 0% -> 0%
where the time goes in v1:
time: 853 us; the launch traced here: 849 us
  waiting for transfers between devices  617 us (72%)
  blocking collectives  102 us (12%)
  matrix products  46.6 us (5%)
  local copies, waits for them, and re-layouts  39.4 us (5%)
  other arithmetic  25.3 us (3%)
  between operations  18.3 us (2%)
    reduce_scatter x3, waiting for transfers between devices, scatter_sum(): lax.psum_scatter(low, BOTH, scatter_dimension=0, tiled=True)  253 us
    all_gather x4, waiting for transfers between devices, general_layer(): lax.all_gather(w, BOTH, axis=0, tiled=True)  188 us
    unnamed x11, waiting for transfers between devices  177 us
    psum x1, blocking collectives, general_layer(): vectors = lax.psum(vectors, BOTH)  41.5 us
    psum x1, blocking collectives, general_layer(): live_count = lax.psum(jnp.sum(live_rows), BOTH)  38.4 us
    dot_general x15, matrix products, mm(): return jnp.einsum(pattern, a, b, preferred_element_type=jnp.float32)  36.7 us
    all_gather x1, blocking collectives, general_layer(): pair_all = lax.all_gather(pair_own, 'blk', axis=1, tiled=True)  22.1 us
  transfers between devices with their start and end apart: 9, of which 9 were waited for; matrix products, arithmetic and copies ran while one was open for 8% of the time, Pallas kernels for 0%

profile of v1, /device:TPU:1, one launch (start us, length us, event | category | flops | bytes accessed | tf_op | source)
XLA Modules:
  0.0 849.3 jit_solution(3981688598094964243)
XLA Ops:
  13.8 1.4 compare_reduce_fusion
  19.8 48.2 %all-gather.5.cloned.1.call-done = bf16[768,896]{1,0:T(8,128)(2,1)} async-done(((bf16[24,896]{1,0:T(8,128)(2,1)}), bf16[768,896]{1,0:T(8,128)(2,1)}) %all-gather.5.cloned.1.call-update) | async-done | bytes 1376272 | tf_op jit(solution)/shard_map/all_gather | solution.py:87
  68.0 1.7 convolution_add_fusion.1
  73.6 22.1 %all_gather.16 = bf16[2,1024,128]{2,0,1:T(2,128)(2,1)S(1)} all-gather(bf16[2,64,128]{2,0,1:T(2,128)(2,1)S(1)} %pad_maximum_fusion.2), channel_id=1, replica_groups=mesh['uly'=2,'blk'=16] {'blk'}, dimensions={1}, use_global_device_ids=true | all-gather | bytes 557056 | tf_op jit(solution)/shard_map/all_gather | solution.py:102
  95.7 1.8 fusion.48
  98.1 7.9 conditional.2
  98.9 2.2 fusion
  101.2 1.8 fusion.2
  103.0 3.0 fusion.8
  108.9 24.7 %all-gather.9.cloned.1.call-done = bf16[768,3072]{1,0:T(8,128)(2,1)} async-done(((bf16[24,3072]{1,0:T(8,128)(2,1)}), bf16[768,3072]{1,0:T(8,128)(2,1)}) %all-gather.9.cloned.1.call-update) | async-done | bytes 4718608 | tf_op jit(solution)/shard_map/all_gather | solution.py:87
  133.7 3.1 convolution_add_fusion
  136.8 62.1 %all-gather.11.cloned.1.call-done = bf16[3072,768]{1,0:T(8,128)(2,1)} async-done(((bf16[96,768]{1,0:T(8,128)(2,1)}), bf16[3072,768]{1,0:T(8,128)(2,1)}) %all-gather.11.cloned.1.call-update) | async-done | bytes 4718608 | tf_op jit(solution)/shard_map/all_gather | solution.py:87
  198.9 3.2 convolution_add_fusion.3
  202.2 52.5 %all-gather.7.cloned.1.call-done = bf16[768,768]{1,0:T(8,128)(2,1)} async-done(((bf16[24,768]{1,0:T(8,128)(2,1)}), bf16[768,768]{1,0:T(8,128)(2,1)}) %all-gather.7.cloned.1.call-update) | async-done | bytes 1179664 | tf_op jit(solution)/shard_map/all_gather | solution.py:87
  254.6 1.8 multiply_reduce_fusion.4
  257.8 38.4 %psum.64 = f32[]{:T(128)} all-reduce(f32[]{:T(128)} %get-tuple-element.293), channel_id=1, replica_groups=mesh['uly'=2,'blk'=16] {'uly','blk'}, use_global_device_ids=true, to_apply=%region_11.12 | all-reduce | flops 1 | bytes 8 | tf_op jit(solution)/shard_map/psum | solution.py:85
  298.7 2.6 convert_multiply_fusion
  301.4 1.9 copy.146
  304.1 1.9 reshape.321
  306.0 2.4 reshape.322
  308.3 1.5 reduce_sum.168
  309.8 16.6 %conditional.3 = (f32[2,64,768]{2,1,0:T(8,128)S(1)}, bf16[2,1024,128]{1,2,0:T(8,128)(2,1)}) conditional(s32[]{:T(128)} %convert_element_type.106, f32[2,64,768]{2,1,0:T(8,128)S(1)} %broadcast.186, (s32[2,1024]{1,0:T(2,128)S(1)}, s32[1,2,12,64]{3,2,1,0:T(8,128)}, bf16[2,1024,64]{2,0,1:T(2,128)(2,1)}, bf16[2,768,64]{1,2,0:T(8,128)(2,1)}, ...), branch_computations={%region_13.14_spmd, %region_14.15_spmd} | conditional | flops 1027147264 | bytes 34705452 | solution.py:205
  310.7 1.9 copy.147
  312.6 2.1 copy.148
  314.7 1.4 reshape.291
  316.1 2.0 fusion.51
  318.1 1.6 fusion.21
  319.8 3.1 multiply_convert_fusion
  323.6 2.0 fusion.20
  327.6 1.8 copy.178
  331.3 2.0 copy.152
  334.5 2.3 pad_maximum_fusion.1
  338.1 1.5 convolution_convert_fusion.3
  339.7 85.1 %all-reduce.5.cloned.1.call-done = bf16[2,1024,128]{2,0,1:T(2,128)(2,1)} async-done(((bf16[2,1024,128]{2,0,1:T(2,128)(2,1)}), bf16[2,1024,128]{2,0,1:T(2,128)(2,1)}) %all-reduce.5.cloned.1.call-update) | async-done | bytes 524304
  428.1 1.6 convolution_convert_fusion.2
  430.0 3.7 convolution_convert_fusion
  433.8 4.2 convert_reduce_fusion
  439.0 3.6 convolution_convert_fusion.1
  443.8 4.2 fusion.52
  449.2 41.5 %all-reduce.2 = (f32[]{:T(128)}, f32[768]{0:T(1024)}, f32[768]{0:T(1024)}, f32[768]{0:T(1024)}, f32[768]{0:T(1024)}, /*index=5*/f32[896]{0:T(1024)}, f32[768]{0:T(1024)S(1)}, f32[3072]{0:T(1024)}) all-reduce(f32[]{:T(128)} %get-tuple-element.294, f32[768]{0:T(1024)S(1)} %get-tuple-element.292, ...), channel_id=1, replica_groups=mesh['uly'=2,'blk'=16] {'uly','blk'}, use_global_device_ids=true, to_apply=%region_9.10 | all-reduce | flops 7809 | bytes 62472 | tf_op jit(solution)/shard_map/psum | solution.py:247
  493.2 31.0 %reduce-scatter.7.cloned.1.call-done = bf16[24,768]{1,0:T(8,128)(2,1)} async-done(((bf16[768,768]{1,0:T(8,128)(2,1)}), bf16[24,768]{1,0:T(8,128)(2,1)}) %reduce-scatter.7.cloned.1.call-update) | async-done | bytes 36880 | tf_op jit(solution)/shard_map/reduce_scatter | solution.py:55
  524.2 1.4 convert_element_type.124
  525.6 89.2 %reduce-scatter.13.cloned.1.call-done = bf16[24,896]{1,0:T(8,128)(2,1)} async-done(((bf16[768,896]{1,0:T(8,128)(2,1)}), bf16[24,896]{1,0:T(8,128)(2,1)}) %reduce-scatter.13.cloned.1.call-update) | async-done | bytes 43024
  614.7 1.4 convert_element_type.121
  616.2 111.6 %reduce-scatter.11.cloned.1.call-done = bf16[96,768]{1,0:T(8,128)(2,1)} async-done(((bf16[3072,768]{1,0:T(8,128)(2,1)}), bf16[96,768]{1,0:T(8,128)(2,1)}) %reduce-scatter.11.cloned.1.call-update) | async-done | bytes 147472 | tf_op jit(solution)/shard_map/reduce_scatter | solution.py:55
  727.8 1.6 convert_element_type.130
  729.4 110.0 %reduce-scatter.9.cloned.1.call-done = bf16[24,3072]{1,0:T(8,128)(2,1)} async-done(((bf16[768,3072]{1,0:T(8,128)(2,1)}), bf16[24,3072]{1,0:T(8,128)(2,1)}) %reduce-scatter.9.cloned.1.call-update) | async-done | bytes 147472 | tf_op jit(solution)/shard_map/reduce_scatter | solution.py:55
  839.4 1.6 convert_element_type.127
  (169 shorter events, 39.0 us)
Async XLA Ops:
  7.2 60.8 %all-gather.5.cloned.1.call-start = ((), (), s32[]{:S(2)}) async-start(), calls=%async_computation.4 | async-start | bytes 1419264 | tf_op jit(solution)/shard_map/all_gather | solution.py:87
  7.9 125.7 %all-gather.9.cloned.1.call-start = ((), (), s32[]{:S(2)}) async-start(), calls=%async_computation.6 | async-start | bytes 4866048 | tf_op jit(solution)/shard_map/all_gather | solution.py:87
  8.7 190.3 %all-gather.11.cloned.1.call-start = ((), (), s32[]{:S(2)}) async-start(), calls=%async_computation.7 | async-start | bytes 4866048 | tf_op jit(solution)/shard_map/all_gather | solution.py:87
  9.4 245.2 %all-gather.7.cloned.1.call-start = ((), (), s32[]{:S(2)}) async-start(), calls=%async_computation.5 | async-start | bytes 1216512 | tf_op jit(solution)/shard_map/all_gather | solution.py:87
  10.0 414.8 %all-reduce.5.cloned.1.call-start = ((), (), s32[]{:S(2)}) async-start(), calls=%async_computation.11 | async-start | bytes 1048576
  11.2 58.8 %copy-start.21 = (f32[128]{0:T(128)}, f32[128]{0:T(128)S(1)}, u32[]{:S(2)}) copy-start(f32[128]{0:T(128)S(1)} %div.62) | copy-start | bytes 1540
  13.1 85.1 %copy-start.17 = (s32[2,1024]{1,0:T(2,128)}, s32[2,1024]{1,0:T(2,128)S(1)}, u32[]{:S(2)}) copy-start(s32[2,1024]{1,0:T(2,128)S(1)} %constant_dynamic-slice_fusion.3) | copy-start | bytes 24580
  16.0 0.5 copy-start.27
  16.5 51.5 %copy-start.23 = (f32[128]{0:T(128)}, f32[128]{0:T(128)S(1)}, u32[]{:S(2)}) copy-start(f32[128]{0:T(128)S(1)} %rsqrt.13) | copy-start | bytes 1540
  19.7 50.8 %copy-start.10 = (bf16[128,768]{1,0:T(8,128)(2,1)}, bf16[128,768]{1,0:T(8,128)(2,1)S(1)}, u32[]{:S(2)}) copy-start(bf16[128,768]{1,0:T(8,128)(2,1)S(1)} %get-tuple-element.319) | copy-start | bytes 589828
  19.7 113.9 %copy-start.5 = (bf16[128,768]{1,0:T(8,128)(2,1)}, bf16[128,768]{1,0:T(8,128)(2,1)S(1)}, u32[]{:S(2)}) copy-start(bf16[128,768]{1,0:T(8,128)(2,1)S(1)} %get-tuple-element.320) | copy-start | bytes 589828
  106.0 27.6 %copy-start.13 = (f32[2,768]{1,0:T(2,128)}, f32[2,768]{1,0:T(2,128)S(1)}, u32[]{:S(2)}) copy-start(f32[2,768]{1,0:T(2,128)S(1)} %get-tuple-element.280) | copy-start | bytes 18436
  106.0 27.6 %copy-start.20 = (f32[3072]{0:T(1024)S(1)}, f32[3072]{0:T(1024)}, u32[]{:S(2)}) copy-start(f32[3072]{0:T(1024)} %param.35) | copy-start | bytes 36868
  133.7 65.3 %copy-start.26 = (f32[768]{0:T(1024)S(1)}, f32[768]{0:T(1024)}, u32[]{:S(2)}) copy-start(f32[768]{0:T(1024)} %param.37) | copy-start | bytes 9220
  136.8 117.8 %copy-start = (bf16[2,64,768]{2,1,0:T(8,128)(2,1)S(1)}, bf16[2,64,768]{2,1,0:T(8,128)(2,1)}, u32[]{:S(2)}) copy-start(bf16[2,64,768]{2,1,0:T(8,128)(2,1)} %param.21) | copy-start | bytes 589828
  136.8 117.8 %copy-start.8 = (bf16[2,64,768]{2,1,0:T(8,128)(2,1)S(1)}, bf16[2,64,768]{2,1,0:T(8,128)(2,1)}, u32[]{:S(2)}) copy-start(bf16[2,64,768]{2,1,0:T(8,128)(2,1)} %param.22) | copy-start | bytes 589828
  298.7 11.1 %copy-start.14 = (f32[2,768]{1,0:T(2,128)S(1)}, f32[2,768]{1,0:T(2,128)}, u32[]{:S(2)}) copy-start(f32[2,768]{1,0:T(2,128)} %copy-done.13) | copy-start | bytes 18436
  298.7 11.1 %copy-start.18 = (s32[2,1024]{1,0:T(2,128)S(1)}, s32[2,1024]{1,0:T(2,128)}, u32[]{:S(2)}) copy-start(s32[2,1024]{1,0:T(2,128)} %copy-done.17) | copy-start | bytes 24580
  298.7 11.1 %copy-start.19 = (f32[2,768]{1,0:T(2,128)S(1)}, f32[2,768]{1,0:T(2,128)}, u32[]{:S(2)}) copy-start(f32[2,768]{1,0:T(2,128)} %log.12) | copy-start | bytes 18436
  319.8 3.1 copy-start.7
  329.5 0.9 copy-start.4
  333.3 94.8 %copy-start.11 = (bf16[128,768]{1,0:T(8,128)(2,1)S(1)}, bf16[128,768]{1,0:T(8,128)(2,1)}, u32[]{:S(2)}) copy-start(bf16[128,768]{1,0:T(8,128)(2,1)} %copy-done.10) | copy-start | bytes 589828
  333.3 190.8 %reduce-scatter.7.cloned.1.call-start = ((), (), s32[]{:S(2)}) async-start(), calls=%async_computation.8 | async-start | bytes 1216512 | tf_op jit(solution)/shard_map/reduce_scatter | solution.py:55
  339.6 275.1 %reduce-scatter.13.cloned.1.call-start = ((), (), s32[]{:S(2)}) async-start(), calls=%async_computation.12 | async-start | bytes 1419264
  429.8 298.0 %reduce-scatter.11.cloned.1.call-start = ((), (), s32[]{:S(2)}) async-start(), calls=%async_computation.10 | async-start | bytes 4866048 | tf_op jit(solution)/shard_map/reduce_scatter | solution.py:55
  433.8 5.2 copy-start.6
  433.8 405.6 %reduce-scatter.9.cloned.1.call-start = ((), (), s32[]{:S(2)}) async-start(), calls=%async_computation.9 | async-start | bytes 4866048 | tf_op jit(solution)/shard_map/reduce_scatter | solution.py:55
  438.1 0.9 copy-start.2
  442.6 1.1 copy-start.3
  443.7 4.4 copy-start.1
  443.7 4.4 copy-start.15
  443.7 4.4 copy-start.16
  443.7 4.4 copy-start.22
  443.7 5.1 copy-start.28
  443.7 5.1 copy-start.24
  447.9 44.1 %copy-start.9 = (bf16[2,64,768]{2,1,0:T(8,128)(2,1)S(1)}, bf16[2,64,768]{2,1,0:T(8,128)(2,1)}, u32[]{:S(2)}) copy-start(bf16[2,64,768]{2,1,0:T(8,128)(2,1)} %param.22) | copy-start | bytes 589828
  447.9 44.1 %copy-start.12 = (bf16[2,64,768]{2,1,0:T(8,128)(2,1)S(1)}, bf16[2,64,768]{2,1,0:T(8,128)(2,1)}, u32[]{:S(2)}) copy-start(bf16[2,64,768]{2,1,0:T(8,128)(2,1)} %param.23) | copy-start | bytes 589828
  490.7 350.9 %copy-start.25 = (f32[768]{0:T(1024)}, f32[768]{0:T(1024)S(1)}, u32[]{:S(2)}) copy-start(f32[768]{0:T(1024)S(1)} %get-tuple-element.377) | copy-start | bytes 9220
Sparse Core Ops, SparseCore 0:
  10.8 57.0 all-gather.4
  70.9 62.7 all-gather.8
  136.6 62.3 all-gather.10
  201.7 52.9 all-gather.6
  333.4 91.3 all-reduce.4
  429.7 94.3 reduce-scatter.6
  529.4 85.2 reduce-scatter.12
  621.1 106.6 reduce-scatter.10
  733.3 106.0 reduce-scatter.8
